TPU v7x, 32 devices: a whole 2x2x4 slice. The times are simulated.
32 devices in a mesh: sect: 2 (over y), op: 16 (over z, x, core).
Axes of the slice: x: 2, y: 2, z: 4, core: 2. Of those that a mesh axis runs over, the one named last changes fastest.
Arguments:
- wave: bfloat16 [2, 8192, 256], P('sect', 'op'), may hold values from -6 to 6
- left_ops: bfloat16 [2, 48, 8, 256, 256], P('sect', 'op'), may hold values from -0.5 to 0.5
- right_ops: bfloat16 [2, 48, 8, 256, 256], P('sect', 'op'), may hold values from -0.375 to 0.375
- site_ops: float32 [2, 48, 4, 4], P('sect', 'op'), may hold values from -0.4375 to 0.4375
- reach: int32 [2, 48], P('sect', 'op'), may hold values from 1 to 8
- pairing: int32 [2, 8], P('sect'), may hold values from 0 to 7, each once within a row
- site_tensor: bfloat16 [2, 8, 4, 256, 256], P('sect'), may hold values from -0.25 to 0.25
Outputs:
- first_image: bfloat16 [2, 8192, 256], P('sect', 'op')
- second_image: bfloat16 [2, 8192, 256], P('sect', 'op')
- moved_image: bfloat16 [2, 8192, 256], P('sect', 'op')
Inputs may be any that keep to these rules, and one draw needn't show every extreme that they name: Each term couples the sectors 0 to reach - 1. `pairing`: each row is a permutation of the 8 sectors.
All inputs are finite; a program needn't handle non-finite values.
Results may differ from a plain program's by a relative error of at most 0.008.
Values may be sent and summed in bfloat16 or wider, within the bound.
A program may use at most 128 MiB of HBM per device.

v0:
```python
import functools

import jax
import jax.numpy as jnp
from jax import lax
from jax.experimental import pallas as pl
from jax.experimental.pallas import tpu as pltpu
from jax.sharding import PartitionSpec as P

VM = pl.BlockSpec(memory_space=pltpu.VMEM)
SUBS = 2
BIG = 67043328


class Ring:
    def __init__(self, count, sections):
        me = lax.axis_index("op")
        here = lax.axis_index("sect")
        self.sections = sections
        self.ahead = {"sect": lax.rem(here + 1, sections)}
        self.behind = {"sect": lax.rem(here + sections - 1, sections)}
        self.m = count // 2
        self.half = self.m // 2
        self.core = lax.rem(me, 2)
        self.chip = lax.div(me, 2)
        odd = lax.rem(self.chip, 2)
        low = lax.div(self.chip, 2)
        self.pos = (1 - odd) * low + odd * (self.m - 1 - low)
        self.sibling = {"op": self.chip * 2 + 1 - self.core}
        self.next = [
            {"op": self.chip_at(1) * 2 + self.core},
            {"op": self.chip_at(-1) * 2 + self.core},
        ]

    def chip_at(self, offset):
        pos = lax.rem(self.pos + offset + self.m, self.m)
        upper = lax.div(pos, self.half)
        return (1 - upper) * (2 * pos) + upper * (2 * (self.m - 1 - pos) + 1)

    def barrier(self):
        sem = pltpu.get_barrier_semaphore()
        peers = [self.next[0], self.next[1], self.sibling, self.ahead]
        if self.sections > 2:
            peers.append(self.behind)
        for who in peers:
            pl.semaphore_signal(sem, inc=1, device_id=who, device_id_type=pl.DeviceIdType.MESH)
        pl.semaphore_wait(sem, len(peers))


def push(src, dst, send, recv, who):
    copy = pltpu.make_async_remote_copy(
        src_ref=src, dst_ref=dst, send_sem=send, recv_sem=recv, device_id=who,
        device_id_type=pl.DeviceIdType.MESH,
    )
    copy.start()
    return copy


def scatter_sum(ring, streams, hook=lambda step: None):
    m, half = ring.m, ring.half
    order = [half]
    for dist in range(half - 1, 0, -1):
        order += [dist, -dist]
    order.append(0)
    sent = []
    sib = {}
    for slot, offset in enumerate(order):
        chunk = ring.chip_at(offset)
        for n, st in enumerate(streams):
            sib[n, offset] = push(
                st["give"].at[chunk], st["land"].at[chunk], st["sib_send"].at[slot],
                st["sib_recv"].at[slot], ring.sibling,
            )
    arrived = set()
    hops = {}

    def local(n, offset, u):
        st = streams[n]
        if (n, offset) not in arrived:
            arrived.add((n, offset))
            sib[n, offset].wait_recv()
        chunk = ring.chip_at(offset)
        rows = st["own"].shape[1] // SUBS
        cut = pl.ds(u * rows, rows)
        return st["own"][chunk, cut, :] + st["land"][chunk, cut, :].astype(jnp.float32)

    def incoming(n, d, j, u):
        hops[n, d, j, u].wait_recv()
        return streams[n]["rbuf"][d, j, u].astype(jnp.float32)

    for j in range(half):
        dist = half - j
        for n, st in enumerate(streams):
            for u in range(SUBS):
                for d in range(2):
                    if dist == half and u != d:
                        continue
                    offset = dist if (d == 0 or dist == half) else -dist
                    value = local(n, offset, u)
                    if (n, d, j - 1, u) in hops:
                        value = value + incoming(n, d, j - 1, u)
                    st["sbuf"][d, j, u] = value.astype(jnp.bfloat16)
                    hops[n, d, j, u] = push(
                        st["sbuf"].at[d, j, u], st["rbuf"].at[d, j, u],
                        st["send"].at[d, j, u], st["recv"].at[d, j, u], ring.next[d],
                    )
        hook(j)
    for n, st in enumerate(streams):
        for u in range(SUBS):
            value = local(n, 0, u)
            for d in range(2):
                if (n, d, half - 1, u) in hops:
                    value = value + incoming(n, d, half - 1, u)
            rows = value.shape[0]
            st["out"][pl.ds(u * rows, rows), :] = value.astype(jnp.bfloat16)
    sent += list(sib.values()) + list(hops.values())
    return sent


def gather(ring, own, whole, send, recv, sib_send, sib_recv, hook):
    half = ring.half
    each = ring.m // whole.shape[0]
    rows = own.shape[0] // SUBS
    sib, hops = [], {}

    def part(chunk, u):
        start = (lax.rem(chunk, each) * 2 + ring.core) * own.shape[0] + u * rows
        return whole.at[lax.div(chunk, each), pl.ds(pl.multiple_of(start, rows), rows)]

    for s in range(half + 1):
        first = len(sib)
        for u in range(SUBS):
            for d in range(2):
                chunk = ring.chip_at(-s if d == 0 else s)
                if s == 0:
                    src = own.at[pl.ds(u * rows, rows)]
                else:
                    if (d, s - 1, u) not in hops:
                        continue
                    hops[d, s - 1, u].wait_recv()
                    src = part(chunk, u)
                if s < half and (s < half - 1 or u == d):
                    hops[d, s, u] = push(
                        src, part(chunk, u), send.at[d, s, u], recv.at[d, s, u], ring.next[d]
                    )
                if s > 0 or d == 0:
                    slot = len(sib)
                    sib.append(push(
                        src, part(chunk, u), sib_send.at[slot], sib_recv.at[slot], ring.sibling
                    ))

        def ready(first=first, last=len(sib)):
            for copy in sib[first:last]:
                copy.wait_recv()

        hook(s, ready)
    return sib + list(hops.values())


def keep_own(ring, own, whole, sem):
    each = ring.m // whole.shape[0]
    start = (lax.rem(ring.chip, each) * 2 + ring.core) * own.shape[0]
    keep = pltpu.make_async_copy(
        own,
        whole.at[lax.div(ring.chip, each), pl.ds(pl.multiple_of(start, own.shape[0]), own.shape[0])],
        sem,
    )
    keep.start()
    return keep


def apply_sector(ring, q, v, left_of, rights, mixers, limits, pair, acc, own, give):
    terms, sectors, block, _ = rights.shape
    local = v.shape[1] // block
    for t in range(terms):
        left = left_of(t, q)
        right = rights[t, pair[q]]
        lifted = [
            jnp.dot(left, v[q, pl.ds(s * block, block), :], preferred_element_type=jnp.float32)
            .astype(jnp.bfloat16).astype(jnp.float32)
            for s in range(local)
        ]
        live = jnp.where(q < limits[t], 1.0, 0.0).astype(jnp.float32)
        for x in range(local):
            mixed = (live * mixers[t, x * local]) * lifted[0]
            for y in range(1, local):
                mixed = mixed + (live * mixers[t, x * local + y]) * lifted[y]
            rows = pl.ds(x * block, block)
            term = lax.dot_general(
                mixed.astype(jnp.bfloat16), right, (((1,), (1,)), ((), ())),
                preferred_element_type=jnp.float32,
            )
            acc[rows, :] = term if t == 0 else acc[rows, :] + term
    rows = own.shape[1]
    each = own.shape[0] // sectors
    for j in range(each):
        mine = pl.multiple_of((2 * j + ring.core) * rows, rows)
        other = pl.multiple_of((2 * j + 1 - ring.core) * rows, rows)
        own[q * each + j] = acc[pl.ds(mine, rows), :]
        give[q * each + j] = acc[pl.ds(other, rows), :].astype(jnp.bfloat16)


def renew_sector(j, back, lefts, tensor, out):
    terms = lefts.shape[0]
    local = tensor.shape[1]
    source = back[j]
    for t in range(terms):
        total = None
        for s in range(local):
            lifted = jnp.dot(
                lefts[t, source], tensor[source, s], preferred_element_type=jnp.float32
            ).astype(jnp.bfloat16)
            term = lax.dot_general(
                tensor[source, s], lifted, (((0,), (0,)), ((), ())),
                preferred_element_type=jnp.float32,
            )
            total = term if total is None else total + term
        out[j, t] = total.astype(jnp.bfloat16)


def while_gathering(ring, sectors, compute, extra=lambda step: None):
    def hook(s, ready):
        extra(s)
        ready()
        if ring.m != sectors:
            if s == ring.half:
                lax.fori_loop(0, sectors, lambda i, c: compute(i) or c, 0)
        elif s == 0 or s == ring.half:
            compute(ring.chip_at(s))
        else:
            lax.fori_loop(0, 2, lambda i, c: compute(ring.chip_at(s * (1 - 2 * i))) or c, 0)

    return hook


def load_all(pairs, sems):
    copies = [pltpu.make_async_copy(a, b, sems.at[i]) for i, (a, b) in enumerate(pairs)]
    for copy in copies:
        copy.start()
    return copies


def stream_of(refs):
    return dict(zip(
        ("own", "give", "out", "land", "sbuf", "rbuf", "send", "recv", "sib_send", "sib_recv"), refs
    ))


def whole_kernel(
    count, sections, pair, back, limits, mixers, wave, left_in, right_in, tensor_in,
    out1, out2, out3,
    lefts, rights, tensor, whole, image, renewed, moved, own_a, own_b, give1, give2, give3, acc,
    loads, local_sem, ahead_send, ahead_recv, *rest
):
    ring = Ring(count, sections)
    loaded = load_all([(left_in, lefts), (tensor_in, tensor), (right_in, rights)], loads)
    keep = keep_own(ring, wave, whole, local_sem.at[0])
    ring.barrier()
    sectors = rights.shape[1]
    per = -(-sectors // ring.half)
    streams = [
        stream_of((own, give, out) + rest[7 * i:7 * i + 7])
        for i, (own, give, out) in enumerate(
            ((own_a, give1, out1), (own_b, give2, out2), (own_a, give3, out3))
        )
    ]
    gather_sems = rest[21:25], rest[25:29]
    crossing = []

    def span(s):
        return min(s * per, sectors), min(s * per + per, sectors)

    def renew_some(s):
        if s == 0:
            for copy in loaded:
                copy.wait()
            keep.wait()
        low, high = span(s)
        if low < high:
            lax.fori_loop(
                low, high, lambda j, c: renew_sector(j, back, lefts, tensor, renewed) or c, 0
            )
        for j in range(low, high):
            crossing.append(push(
                renewed.at[j], moved.at[j], ahead_send.at[j], ahead_recv.at[j], ring.ahead
            ))

    def apply_first(q):
        apply_sector(
            ring, q, whole, lambda t, q: lefts[t, q], rights, mixers, limits, pair, acc,
            own_a, give1,
        )

    def apply_second(q):
        apply_sector(
            ring, q, image, lambda t, q: lefts[t, q], rights, mixers, limits, pair, acc,
            own_b, give2,
        )

    def apply_moved(s):
        low, high = span(s)
        for j in range(low, high):
            crossing[j].wait_recv()

        def body(q, c):
            apply_sector(
                ring, q, whole, lambda t, q: moved[q, t], rights, mixers, limits, pair, acc,
                own_a, give3,
            )
            return c

        if low < high:
            lax.fori_loop(low, high, body, 0)

    sent = gather(
        ring, wave, whole, *gather_sems[0],
        while_gathering(ring, sectors, apply_first, renew_some),
    )
    sent += scatter_sum(ring, streams[:1])
    kept = keep_own(ring, out1, image, local_sem.at[1])

    def settle(s):
        if s == 0:
            kept.wait()

    sent += gather(
        ring, out1, image, *gather_sems[1],
        while_gathering(ring, sectors, apply_second, settle),
    )
    sent += scatter_sum(ring, streams[1:2], apply_moved)
    sent += scatter_sum(ring, streams[2:])
    for copy in sent + crossing:
        copy.wait_send()


def gather_scratch(count):
    half = count // 4
    dma = pltpu.SemaphoreType.DMA
    slots = SUBS * (2 * half)
    return [dma((2, half, SUBS)), dma((2, half, SUBS)), dma((slots,)), dma((slots,))]


def stream_scratch(chips, rows, width):
    half = chips // 2
    dma = pltpu.SemaphoreType.DMA
    hop = (2, half, SUBS, rows // SUBS, width)
    return [
        pltpu.VMEM((chips, rows, width), jnp.bfloat16),
        pltpu.VMEM(hop, jnp.bfloat16),
        pltpu.VMEM(hop, jnp.bfloat16),
        dma((2, half, SUBS)), dma((2, half, SUBS)), dma((chips,)), dma((chips,)),
    ]


def shards(count, sections, wave, left_ops, right_ops, site_ops, reach, pairing, site_tensor):
    lefts, rights, limits, pair = left_ops[0], right_ops[0], reach[0], pairing[0]
    mixers = site_ops[0].reshape(site_ops.shape[1], -1)
    own, tensor = wave[0], site_tensor[0]
    sectors, block = lefts.shape[1:3]
    ids = jnp.arange(sectors, dtype=jnp.int32)
    back = jnp.sum((pair[None, :] == ids[:, None]) * ids[None, :], axis=1).astype(jnp.int32)
    rows, width = own.shape
    chips = count // 2
    height = count * rows // sectors
    dma = pltpu.SemaphoreType.DMA
    sm = pl.BlockSpec(memory_space=pltpu.SMEM)
    anyw = pl.BlockSpec(memory_space=pl.ANY)
    bf, f32 = jnp.bfloat16, jnp.float32
    image = pltpu.VMEM((sectors, height, width), bf)
    total = pltpu.VMEM((chips, rows, width), f32)
    give = pltpu.VMEM((chips, rows, width), bf)
    across = pltpu.VMEM((sectors, lefts.shape[0], block, block), bf)
    mine = jax.ShapeDtypeStruct((rows, width), bf)
    outs = pl.pallas_call(
        functools.partial(whole_kernel, count, sections),
        out_shape=[mine] * 3,
        in_specs=[sm] * 4 + [VM] + [anyw] * 3,
        out_specs=[VM] * 3,
        scratch_shapes=[
            pltpu.VMEM(lefts.shape, bf), pltpu.VMEM(rights.shape, bf),
            pltpu.VMEM(tensor.shape, bf), image, image, across, across, total, total,
            give, give, give, pltpu.VMEM((height, width), f32),
            dma((3,)), dma((2,)), dma((sectors,)), dma((sectors,)),
        ] + stream_scratch(chips, rows, width) * 3 + gather_scratch(count) * 2,
        compiler_params=pltpu.CompilerParams(
            collective_id=0, has_side_effects=True, vmem_limit_bytes=BIG
        ),
        name="images",
    )(pair, back, limits, mixers, own, lefts, rights, tensor)
    return tuple(out[None] for out in outs)


def solution(mesh):
    placed = (
        P("sect", "op", None),
        P("sect", "op", None, None, None),
        P("sect", "op", None, None, None),
        P("sect", "op", None, None),
        P("sect", "op"),
        P("sect", None),
        P("sect", None, None, None, None),
    )
    return jax.shard_map(
        functools.partial(shards, mesh.shape["op"], mesh.shape["sect"]),
        mesh=mesh,
        in_specs=placed,
        out_specs=(P("sect", "op", None), P("sect", "op", None), P("sect", "op", None)),
        check_vma=False,
    )
```

profile of v0, /device:TPU:0, one launch (start us, length us, event | category | flops | bytes accessed | tf_op | source)
XLA Modules:
  0.0 144.1 jit_solution(2264711875962179009)
XLA Ops:
  0.6 1.3 select_reduce_fusion.back
  1.9 1.4 reshape_squeeze.3.mixers
  3.3 135.8 %images.1 = (bf16[512,256]{1,0:T(8,128)(2,1)}, bf16[512,256]{1,0:T(8,128)(2,1)}, bf16[512,256]{1,0:T(8,128)(2,1)}) custom-call(s32[8]{0:T(128)} %bitcast.17, s32[8]{0:T(128)} %select_reduce_fusion.back, s32[3]{0:T(128)} %bitcast.18, f32[3,16]{1,0:T(4,128)} %reshape_squeeze.3.mixers, bf16[512,256]{1,0:T(8,128)(2,1)} %bitcast.12, ...), custom_call_target="tpu_custom_call" | custom-call | tf_op jit(solution)/shard_map/images/pallas_call | solution.py:374
  139.1 1.7 %copy.13 = bf16[1,512,256]{2,1,0:T(8,128)(2,1)} copy(bf16[1,512,256]{2,1,0:T(8,128)(2,1)} %bitcast.15) | data formatting | bytes 524288
  140.7 1.7 %copy.14 = bf16[1,512,256]{2,1,0:T(8,128)(2,1)} copy(bf16[1,512,256]{2,1,0:T(8,128)(2,1)} %bitcast.14) | data formatting | bytes 524288
  142.4 1.7 %copy.15 = bf16[1,512,256]{2,1,0:T(8,128)(2,1)} copy(bf16[1,512,256]{2,1,0:T(8,128)(2,1)} %bitcast.13) | data formatting | bytes 524288
where the time goes:
time: 144 us
  Pallas kernels  136 us (94%)
  local copies, waits for them, and re-layouts  6.36 us (4%)
    pallas_call x1, Pallas kernels, shards(): pl.pallas_call(functools.partial(whole_kernel, count, sections), out_shap...  136 us
    unnamed x3, local copies, waits for them, and re-layouts  5.01 us

commit v1 on v0

v1 whole, which is shorter than its diff:
```python
import functools

import jax
import jax.numpy as jnp
from jax import lax
from jax.experimental import pallas as pl
from jax.experimental.pallas import tpu as pltpu
from jax.sharding import PartitionSpec as P

SUBS = 2
BIG = 67043328
BF, F32 = jnp.bfloat16, jnp.float32


def remote(src, dst, send, recv, who):
    return pltpu.make_async_remote_copy(
        src_ref=src, dst_ref=dst, send_sem=send, recv_sem=recv, device_id=who,
        device_id_type=pl.DeviceIdType.MESH,
    )


def cond(test, body):
    if isinstance(test, bool):
        if test:
            body()
    else:
        pl.when(test)(body)


def both(a, b):
    return (a and b) if isinstance(a, bool) and isinstance(b, bool) else jnp.logical_and(a, b)


def either(a, b):
    return (a or b) if isinstance(a, bool) and isinstance(b, bool) else jnp.logical_or(a, b)


def loop(low, high, body):
    if low < high:
        lax.fori_loop(low, high, lambda i, c: body(i) or c, 0)


class Ring:
    def __init__(self, count, sections):
        me = lax.axis_index("op")
        here = lax.axis_index("sect")
        self.sections = sections
        self.ahead = {"sect": lax.rem(here + 1, sections)}
        self.behind = {"sect": lax.rem(here + sections - 1, sections)}
        self.m = count // 2
        self.half = self.m // 2
        self.core = lax.rem(me, 2)
        self.chip = lax.div(me, 2)
        odd = lax.rem(self.chip, 2)
        low = lax.div(self.chip, 2)
        self.pos = (1 - odd) * low + odd * (self.m - 1 - low)
        self.sibling = {"op": self.chip * 2 + 1 - self.core}
        self.next = [
            {"op": self.chip_at(1) * 2 + self.core},
            {"op": self.chip_at(-1) * 2 + self.core},
        ]

    def chip_at(self, offset):
        pos = lax.rem(self.pos + offset + self.m, self.m)
        upper = lax.div(pos, self.half)
        return (1 - upper) * (2 * pos) + upper * (2 * (self.m - 1 - pos) + 1)

    def chip_of(self, n):
        if isinstance(n, int):
            return self.chip_at((n + 1) // 2 * (2 * (n % 2) - 1))
        return self.chip_at(lax.div(n + 1, 2) * (2 * lax.rem(n, 2) - 1))

    def barrier(self):
        sem = pltpu.get_barrier_semaphore()
        peers = [self.next[0], self.next[1], self.sibling, self.ahead]
        if self.sections > 2:
            peers.append(self.behind)
        for who in peers:
            pl.semaphore_signal(sem, inc=1, device_id=who, device_id_type=pl.DeviceIdType.MESH)
        pl.semaphore_wait(sem, len(peers))


class Gather:
    def __init__(self, ring, whole, rows, sems):
        self.ring, self.whole, self.rows = ring, whole, rows
        self.send, self.recv, self.sib_send, self.sib_recv = sems
        self.each = ring.m // whole.shape[0]

    def at(self, chunk, first, size):
        start = (lax.rem(chunk, self.each) * 2 + self.ring.core) * self.rows + first
        return self.whole.at[lax.div(chunk, self.each), pl.ds(pl.multiple_of(start, size), size)]

    def part(self, chunk, u):
        return self.at(chunk, u * (self.rows // SUBS), self.rows // SUBS)

    def own(self):
        return self.at(self.ring.chip, 0, self.rows)

    def hop(self, d, s, u, ref):
        return remote(ref, ref, self.send.at[d, s, u], self.recv.at[d, s, u], self.ring.next[d])

    def over(self, d, s, u, ref):
        return remote(
            ref, ref, self.sib_send.at[d, s, u], self.sib_recv.at[d, s, u], self.ring.sibling
        )

    def start(self, u):
        ref = self.part(self.ring.chip, u)
        for d in range(2):
            if self.ring.half > 1 or u == d:
                self.hop(d, 0, u, ref).start()
        self.over(0, 0, u, ref).start()

    def forward(self, s, u):
        half = self.ring.half
        for d in range(2):
            ref = self.part(self.ring.chip_at(-s if d == 0 else s), u)

            def pass_on(d=d, ref=ref):
                self.hop(d, s - 1, u, ref).wait_recv()
                cond(
                    both(s < half, either(s < half - 1, u == d)),
                    lambda: self.hop(d, s, u, ref).start(),
                )
                self.over(d, s, u, ref).start()

            cond(either(s < half, u == d), pass_on)

    def ready(self, n):
        m, half = self.ring.m, self.ring.half
        ref = self.part(self.ring.chip, 0)

        def far():
            for d in range(2):
                self.over(d, half, d, ref).wait_recv()

        def near():
            d, s = lax.rem(n, 2), lax.div(n + 1, 2)
            for u in range(SUBS):
                self.over(d, s, u, ref).wait_recv()

        pl.when(n == m - 1)(far)
        pl.when(n != m - 1)(near)

    def run(self, work):
        m = self.ring.m

        def body(i):
            pl.when(i < m)(lambda: self.forward(lax.div(i, 2) + 1, lax.rem(i, 2)))

            def at(n):
                self.ready(n)

            n = jnp.maximum(i - 1, 0)
            work(i, n, lambda: pl.when(i != 1)(lambda: at(n)))

        loop(0, m + 1, body)

    def drain(self):
        half = self.ring.half
        ref = self.part(self.ring.chip, 0)
        for d in range(2):
            for u in range(SUBS):
                for s in range(half + 1):
                    if s < half and (s < half - 1 or u == d):
                        self.hop(d, s, u, ref).wait_send()
                    if (d == 0) if s == 0 else (s < half or u == d):
                        self.over(d, s, u, ref).wait_send()


class Scatter:
    def __init__(self, ring, own, give, land, buf, sems):
        self.ring, self.own, self.give, self.land, self.buf = ring, own, give, land, buf
        self.send, self.recv, self.sib_send, self.sib_recv = sems
        self.rows = own.shape[1] // SUBS

    def over(self, n, chunk):
        return remote(
            self.give.at[chunk], self.land.at[chunk], self.sib_send.at[n], self.sib_recv.at[n],
            self.ring.sibling,
        )

    def offer(self, n):
        self.over(n, self.ring.chip_of(n)).start()

    def settle(self, n):
        self.over(n, self.ring.chip).wait_recv()

    def move(self, d, j, u):
        return remote(
            self.buf.at[d, j, u], self.buf.at[d, j + 1, u], self.send.at[d, j, u],
            self.recv.at[d, j, u], self.ring.next[d],
        )

    def local(self, chunk, u):
        cut = pl.ds(pl.multiple_of(u * self.rows, self.rows), self.rows)
        return self.own[chunk, cut, :] + self.land[chunk, cut, :].astype(F32)

    def first(self):
        m, half = self.ring.m, self.ring.half
        self.settle(m - 1)
        for d in range(2):
            self.buf[d, 0, d] = self.local(self.ring.chip_at(half), d).astype(BF)
            self.move(d, 0, d).start()

    def hop(self, j, u):
        dist = self.ring.half - j

        def settle():
            self.settle(2 * dist - 1)
            self.settle(2 * dist)

        cond(u == 0, settle)
        for d in range(2):
            value = self.local(self.ring.chip_at(dist if d == 0 else -dist), u)
            has = either(j > 1, u == d)

            def add(d=d, value=value):
                self.move(d, j - 1, u).wait_recv()
                self.buf[d, j, u] = (value + self.buf[d, j, u].astype(F32)).astype(BF)

            def put(d=d, value=value):
                self.buf[d, j, u] = value.astype(BF)

            cond(has, add)
            cond((not has) if isinstance(has, bool) else jnp.logical_not(has), put)
            self.move(d, j, u).start()

    def last(self, u):
        half = self.ring.half
        if u == 0:
            self.settle(0)
        value = self.local(self.ring.chip, u)
        for d in range(2):
            if half > 1 or u == d:
                self.move(d, half - 1, u).wait_recv()
                value = value + self.buf[d, half, u].astype(F32)
        return value.astype(BF)

    def drain(self):
        for d in range(2):
            for u in range(SUBS):
                for j in range(self.ring.half):
                    if j or u == d:
                        self.move(d, j, u).wait_send()
        for n in range(self.ring.m):
            self.over(n, self.ring.chip).wait_send()


class Apply:
    def __init__(self, ring, rights, mixers, limits, pair, acc):
        self.ring, self.rights, self.acc = ring, rights, acc
        self.mixers, self.limits, self.pair = mixers, limits, pair
        self.terms, self.sectors, self.block, _ = rights.shape
        self.local = mixers.shape[2]

    def lift(self, t, q, left, v):
        return [
            jnp.dot(left, v[q, pl.ds(s * self.block, self.block), :], preferred_element_type=F32)
            .astype(BF)
            for s in range(self.local)
        ]

    def mix(self, t, q, x, lifted):
        live = jnp.where(q < self.limits[0, t], 1.0, 0.0).astype(F32)
        mixed = (live * self.mixers[0, t, x, 0]) * lifted[0].astype(F32)
        for y in range(1, self.local):
            mixed = mixed + (live * self.mixers[0, t, x, y]) * lifted[y].astype(F32)
        return mixed.astype(BF)

    def right(self, t, q, mixed):
        return lax.dot_general(
            mixed, self.rights[t, self.pair[0, q]], (((1,), (1,)), ((), ())),
            preferred_element_type=F32,
        )

    def to(self, q, v, left_of, st, given):
        per = self.local // 2
        lifted = [self.lift(t, q, left_of(t), v) for t in range(self.terms)]
        for i in range(self.local):
            core = 1 - self.ring.core if i < per else self.ring.core
            x = core * per + i % per
            total = None
            for t in range(self.terms):
                term = self.right(t, q, self.mix(t, q, x, lifted[t]))
                total = term if total is None else total + term
            rows = pl.ds(i % per * self.block, self.block)
            if i < per:
                st.give[q, rows, :] = total.astype(BF)
            else:
                st.own[q, rows, :] = total
            if i == per - 1:
                given()

    def shared(self, q, v, left_of, st):
        acc = self.acc
        for t in range(self.terms):
            lifted = self.lift(t, q, left_of(t), v)
            for x in range(self.local):
                rows = pl.ds(x * self.block, self.block)
                term = self.right(t, q, self.mix(t, q, x, lifted))
                acc[rows, :] = term if t == 0 else acc[rows, :] + term
        rows = st.own.shape[1]
        each = st.own.shape[0] // self.sectors
        core = self.ring.core
        for j in range(each):
            mine = pl.multiple_of((2 * j + core) * rows, rows)
            other = pl.multiple_of((2 * j + 1 - core) * rows, rows)
            st.own[q * each + j] = acc[pl.ds(mine, rows), :]
            st.give[q * each + j] = acc[pl.ds(other, rows), :].astype(BF)


def renew(i, j, pair, lefts, tensor, out):
    terms, sectors = lefts.shape[:2]
    local = tensor.shape[1]
    source = jnp.int32(0)
    for k in range(sectors):
        source = jnp.where(pair[0, k] == j, k, source)
    stack = jnp.concatenate([tensor[source, s] for s in range(local)], axis=0)
    for t in range(terms):
        lifted = [
            jnp.dot(lefts[t, source], tensor[source, s], preferred_element_type=F32).astype(BF)
            for s in range(local)
        ]
        out[i, t] = lax.dot_general(
            stack, jnp.concatenate(lifted, axis=0), (((0,), (0,)), ((), ())),
            preferred_element_type=F32,
        ).astype(BF)


def interleaved(chips, sectors, local):
    return chips == sectors and chips > 6 and local % 2 == 0


def whole_kernel(
    count, sections, pair, limits, mixers, wave, left_in, right_in, tensor_in,
    out1, out2, out3,
    lefts, rights, tensor, whole, image, renewed, moved, acc, stage,
    loads, writes, cross_send, cross_recv, *rest
):
    ring = Ring(count, sections)
    m, half, core = ring.m, ring.half, ring.core
    terms, sectors = rights.shape[:2]
    rows = wave.shape[0]
    tight = interleaved(m, sectors, mixers.shape[2])
    s1, s2, s3 = (
        Scatter(ring, *rest[8 * i:8 * i + 4], rest[8 * i + 4:8 * i + 8]) for i in range(3)
    )
    g1 = Gather(ring, whole, rows, rest[24:28])
    g2 = Gather(ring, image, rows, rest[28:32])
    work = Apply(ring, rights, mixers, limits, pair, acc)

    keep = pltpu.make_async_copy(wave, g1.own(), loads.at[3])
    keep.start()
    ring.barrier()
    keep.wait()
    for u in range(SUBS):
        g1.start(u)
    loaded = [
        pltpu.make_async_copy(a, b, loads.at[i])
        for i, (a, b) in enumerate(((left_in, lefts), (tensor_in, tensor), (right_in, rights)))
    ]
    for copy in loaded:
        copy.start()

    def sector_of(i):
        return ring.chip_of(m - 1 - i) if tight else i

    def crossing(i):
        return remote(
            renewed.at[i], moved.at[i], cross_send.at[i], cross_recv.at[i], ring.ahead
        )

    def renew_one(i):
        renew(i, sector_of(i), pair, lefts, tensor, renewed)
        crossing(i).start()

    def apply_to(st, v, n):
        work.to(ring.chip_of(n), v, lambda t: lefts[t, ring.chip_of(n)], st, lambda: st.offer(n))

    def apply_moved(i):
        crossing(i).wait_recv()
        n = m - 1 - i
        work.to(ring.chip_of(n), whole, lambda t: moved[i, t], s3, lambda: s3.offer(n))

    def hops(st, low, high, slot):
        def body(k):
            pl.when(k > low)(
                lambda: st.hop(1 + lax.div(k - low - 1, SUBS), lax.rem(k - low - 1, SUBS))
            )
            slot(k)

        loop(low, high, body)

    def finish(st, ref, after=lambda u: None):
        size = rows // SUBS
        for u in range(SUBS):
            ref[pl.ds(u * size, size), :] = st.last(u)
            after(u)

    def write(i, src, dst):
        pltpu.make_async_copy(src, dst, writes.at[i]).start()

    for copy in loaded:
        copy.wait()
    steps = SUBS * (half - 1) + 1
    if tight:
        def first_work(i, n, ready):
            pl.when(jnp.logical_or(i == 0, jnp.logical_and(lax.rem(i, 2) == 1, i < m - 1)))(
                lambda: renew_one(lax.div(i + 1, 2))
            )
            ready()
            pl.when(i != 1)(lambda: apply_to(s1, whole, n))

        g1.run(first_work)
        s1.first()

        def first_slot(k):
            pl.when(jnp.logical_and(k > 0, k <= half))(lambda: renew_one(half - 1 + k))
            pl.when(jnp.logical_or(k == 0, jnp.logical_and(k > half, k <= half + 2)))(
                lambda: apply_moved(jnp.maximum(k - half, 0))
            )
            pl.when(k == 0)(s3.first)

        hops(s1, 0, steps, first_slot)
        for u in range(SUBS):
            s3.hop(1, u)
        finish(s1, g2.own(), g2.start)
        write(0, g2.own(), out1)

        def second_work(i, n, ready):
            pl.when(i == m - 2)(lambda: [s3.hop(2, u) for u in range(SUBS)] and None)
            ready()
            pl.when(i != 1)(lambda: apply_to(s2, image, n))
            pl.when(jnp.logical_and(lax.rem(i, 2) == 1, i < m - 1))(
                lambda: apply_moved(3 + lax.div(i, 2))
            )

        g2.run(second_work)
        s2.first()
        done = half + 2

        def second_slot(k):
            pl.when(jnp.logical_and(lax.rem(k, 2) == 0, k < 2 * (sectors - done)))(
                lambda: apply_moved(done + lax.div(k, 2))
            )
            for j in range(3, half):
                pl.when(k == max(2 * (2 * j - done) + 1, 1))(
                    lambda j=j: [s3.hop(j, u) for u in range(SUBS)] and None
                )

        hops(s2, 0, steps, second_slot)
        finish(s3, stage.at[1])
        write(2, stage.at[1], out3)
        finish(s2, stage.at[0])
        write(1, stage.at[0], out2)
    else:
        def plain(i, n, ready):
            ready()

        def spread(st, v, left_of, before=lambda q: None):
            def body(q):
                before(q)
                work.shared(q, v, functools.partial(left_of, q), st)

            loop(0, sectors, body)
            loop(0, m, st.offer)
            st.first()
            hops(st, 0, steps, lambda k: None)

        def plain_left(q, t):
            return lefts[t, q]

        loop(0, sectors, renew_one)
        g1.run(plain)
        spread(s1, whole, plain_left)
        finish(s1, g2.own(), g2.start)
        write(0, g2.own(), out1)
        g2.run(plain)
        spread(s2, image, plain_left)
        finish(s2, stage.at[0])
        write(1, stage.at[0], out2)
        spread(s3, whole, lambda q, t: moved[q, t], lambda q: crossing(q).wait_recv())
        finish(s3, stage.at[1])
        write(2, stage.at[1], out3)
    for part in (g1, g2, s1, s2, s3):
        part.drain()
    loop(0, sectors, lambda i: crossing(i).wait_send())
    for i, out in enumerate((out1, out2, out3)):
        pltpu.make_async_copy(stage.at[0], out, writes.at[i]).wait()


def hand_out(*refs):
    ins, outs, (held, loads, writes) = refs[:3], refs[3:6], refs[6:]
    copies = [pltpu.make_async_copy(a, held.at[i], loads.at[i]) for i, a in enumerate(ins)]
    for copy in copies:
        copy.start()
    back = []
    for i, copy in enumerate(copies):
        copy.wait()
        back.append(pltpu.make_async_copy(held.at[i], outs[i], writes.at[i]))
        back[-1].start()
    for copy in back:
        copy.wait()


def gather_scratch(half):
    dma = pltpu.SemaphoreType.DMA
    hop, sib = (2, half, SUBS), (2, half + 1, SUBS)
    return [dma(hop), dma(hop), dma(sib), dma(sib)]


def scatter_scratch(chips, rows, width):
    half = chips // 2
    dma = pltpu.SemaphoreType.DMA
    hop = (2, half, SUBS)
    return [
        pltpu.VMEM((chips, rows, width), F32),
        pltpu.VMEM((chips, rows, width), BF),
        pltpu.VMEM((chips, rows, width), BF),
        pltpu.VMEM((2, half + 1, SUBS, rows // SUBS, width), BF),
        dma(hop), dma(hop), dma((chips,)), dma((chips,)),
    ]


def shards(count, sections, wave, left_ops, right_ops, site_ops, reach, pairing, site_tensor):
    lefts, rights, own, tensor = left_ops[0], right_ops[0], wave[0], site_tensor[0]
    terms, sectors, block, _ = lefts.shape
    rows, width = own.shape
    chips = count // 2
    height = count * rows // sectors
    tight = interleaved(chips, sectors, site_ops.shape[2])
    dma = pltpu.SemaphoreType.DMA
    sm = pl.BlockSpec(memory_space=pltpu.SMEM)
    anyw = pl.BlockSpec(memory_space=pl.ANY)
    image = pltpu.VMEM((sectors, height, width), BF)
    across = pltpu.VMEM((sectors, terms, block, block), BF)
    mine = jax.ShapeDtypeStruct((rows, width), BF)
    outs = pl.pallas_call(
        functools.partial(whole_kernel, count, sections),
        out_shape=[mine] * 3,
        in_specs=[sm] * 3 + [anyw] * 4,
        out_specs=[anyw] * 3,
        scratch_shapes=[
            pltpu.VMEM(lefts.shape, BF), pltpu.VMEM(rights.shape, BF),
            pltpu.VMEM(tensor.shape, BF), image, image, across, across,
            pltpu.VMEM((8, width) if tight else (height, width), F32),
            pltpu.VMEM((2, rows, width), BF),
            dma((4,)), dma((3,)), dma((sectors,)), dma((sectors,)),
        ] + scatter_scratch(chips, rows, width) * 3 + gather_scratch(chips // 2) * 2,
        compiler_params=pltpu.CompilerParams(
            collective_id=0, has_side_effects=True, vmem_limit_bytes=BIG
        ),
        name="images",
    )(pairing, reach, site_ops, own, lefts, rights, tensor)
    outs = pl.pallas_call(
        hand_out,
        out_shape=[mine] * 3,
        in_specs=[anyw] * 3,
        out_specs=[anyw] * 3,
        scratch_shapes=[pltpu.VMEM((3, rows, width), BF), dma((3,)), dma((3,))],
        name="hand_out",
    )(*outs)
    return tuple(out[None] for out in outs)


def solution(mesh):
    placed = (
        P("sect", "op", None),
        P("sect", "op", None, None, None),
        P("sect", "op", None, None, None),
        P("sect", "op", None, None),
        P("sect", "op"),
        P("sect", None),
        P("sect", None, None, None, None),
    )
    return jax.shard_map(
        functools.partial(shards, mesh.shape["op"], mesh.shape["sect"]),
        mesh=mesh,
        in_specs=placed,
        out_specs=(P("sect", "op", None), P("sect", "op", None), P("sect", "op", None)),
        check_vma=False,
    )
```

time: 144 us -> 126 us (0.88)
  Pallas kernels: 136 us -> 125 us
  local copies, waits for them, and re-layouts: 6.36 us -> 0 us
    pallas_call x1, Pallas kernels: 136 us -> 123 us  [shards(): pl.pallas_call(functools.partial(whole_kernel, count, sections), out_shap...]
    unnamed x3 -> x0, local copies, waits for them, and re-layouts: 5.01 us -> none
    pallas_call x0 -> x1, Pallas kernels: none -> 1.88 us  [shards(): pl.pallas_call(hand_out, out_shape=[mine] * 3, in_specs=[anyw] * 3, out_s...]
where the time goes in v1:
time: 126 us; the launch traced here: 125 us
  Pallas kernels  125 us (99%)
    pallas_call x1, Pallas kernels, shards(): pl.pallas_call(functools.partial(whole_kernel, count, sections), out_shap...  123 us

profile of v1, /device:TPU:0, one launch (start us, length us, event | category | flops | bytes accessed | tf_op | source)
XLA Modules:
  0.0 125.4 jit_solution(4291855512925162209)
XLA Ops:
  0.6 122.9 %images.1 = (bf16[512,256]{1,0:T(8,128)(2,1)}, bf16[512,256]{1,0:T(8,128)(2,1)}, bf16[512,256]{1,0:T(8,128)(2,1)}) custom-call(s32[1,8]{1,0:T(1,128)} %pair.1, s32[1,3]{1,0:T(1,128)} %limits.1, f32[1,3,4,4]{3,2,1,0:T(4,128)} %mixers.1, bf16[512,256]{1,0:T(8,128)(2,1)} %bitcast.10, bf16[3,8,256,256]{3,2,1,0:T(8,128)(2,1)} %bitcast.8, ...), custom_call_target="tpu_custom_call" | custom-call | tf_op jit(solution)/shard_map/images/pallas_call | solution.py:539
  123.5 1.9 %hand_out.1 = (bf16[512,256]{1,0:T(8,128)(2,1)}, bf16[512,256]{1,0:T(8,128)(2,1)}, bf16[512,256]{1,0:T(8,128)(2,1)}) custom-call(bf16[512,256]{1,0:T(8,128)(2,1)} %get-tuple-element.9.refs_0_, bf16[512,256]{1,0:T(8,128)(2,1)} %get-tuple-element.10.refs_1_, bf16[512,256]{1,0:T(8,128)(2,1)} %get-tuple-element.11.refs_2_), custom_call_target="tpu_custom_call" | custom-call | tf_op jit(solution)/shard_map/hand_out/pallas_call | solution.py:556

commit v2 on v1

--- a/solution.py
+++ b/solution.py
@@ -105,26 +105,29 @@
         )
 
     def start(self, u):
-        ref = self.part(self.ring.chip, u)
-        for d in range(2):
-            if self.ring.half > 1 or u == d:
-                self.hop(d, 0, u, ref).start()
-        self.over(0, 0, u, ref).start()
-
-    def forward(self, s, u):
+        half = self.ring.half
+        refs = [self.part(self.ring.chip, v) for v in range(SUBS)]
+        self.hop(u, 0, u, refs[u]).start()
+        self.over(0, 0, u, refs[u]).start()
+        if u and half > 1:
+            for d in range(2):
+                self.hop(d, 0, 1 - d, refs[1 - d]).start()
+
+    def forward(self, s, v):
         half = self.ring.half
         for d in range(2):
+            u = v if d == 0 else 1 - v
             ref = self.part(self.ring.chip_at(-s if d == 0 else s), u)
 
-            def pass_on(d=d, ref=ref):
+            def pass_on(d=d, u=u, ref=ref):
                 self.hop(d, s - 1, u, ref).wait_recv()
                 cond(
-                    both(s < half, either(s < half - 1, u == d)),
+                    both(s < half, either(s < half - 1, v == 0)),
                     lambda: self.hop(d, s, u, ref).start(),
                 )
                 self.over(d, s, u, ref).start()
 
-            cond(either(s < half, u == d), pass_on)
+            cond(either(s < half, v == 0), pass_on)
 
     def ready(self, n):
         m, half = self.ring.m, self.ring.half
@@ -146,15 +149,12 @@
         m = self.ring.m
 
         def body(i):
-            pl.when(i < m)(lambda: self.forward(lax.div(i, 2) + 1, lax.rem(i, 2)))
-
-            def at(n):
-                self.ready(n)
-
-            n = jnp.maximum(i - 1, 0)
-            work(i, n, lambda: pl.when(i != 1)(lambda: at(n)))
-
-        loop(0, m + 1, body)
+            self.forward(lax.div(i, 2) + 1, lax.rem(i, 2))
+            low = jnp.where(i > m - 3, i, jnp.maximum(i - 1, 0))
+            many = jnp.where(i == 1, 0, jnp.where(i == m - 3, 2, 1))
+            work(i, low, low + many)
+
+        loop(0, m, body)
 
     def drain(self):
         half = self.ring.half
@@ -196,35 +196,37 @@
         cut = pl.ds(pl.multiple_of(u * self.rows, self.rows), self.rows)
         return self.own[chunk, cut, :] + self.land[chunk, cut, :].astype(F32)
 
-    def first(self):
+    def step(self, j, late):
         m, half = self.ring.m, self.ring.half
-        self.settle(m - 1)
-        for d in range(2):
-            self.buf[d, 0, d] = self.local(self.ring.chip_at(half), d).astype(BF)
-            self.move(d, 0, d).start()
-
-    def hop(self, j, u):
-        dist = self.ring.half - j
-
-        def settle():
+        dist = half - j
+        if isinstance(j, int) and j == 0:
+            self.settle(m - 1)
+        elif not late:
             self.settle(2 * dist - 1)
             self.settle(2 * dist)
-
-        cond(u == 0, settle)
+        fresh = isinstance(j, int) and j == (0 if late else 1)
         for d in range(2):
+            u = d if late else 1 - d
             value = self.local(self.ring.chip_at(dist if d == 0 else -dist), u)
-            has = either(j > 1, u == d)
-
-            def add(d=d, value=value):
+            if not fresh:
                 self.move(d, j - 1, u).wait_recv()
-                self.buf[d, j, u] = (value + self.buf[d, j, u].astype(F32)).astype(BF)
-
-            def put(d=d, value=value):
-                self.buf[d, j, u] = value.astype(BF)
-
-            cond(has, add)
-            cond((not has) if isinstance(has, bool) else jnp.logical_not(has), put)
+                value = value + self.buf[d, j, u].astype(F32)
+            self.buf[d, j, u] = value.astype(BF)
             self.move(d, j, u).start()
+
+    def rest(self, slot, before=lambda q: None):
+        half = self.ring.half
+
+        def body(q):
+            k = lax.div(q, 2)
+            before(q)
+            pl.when(jnp.logical_and(lax.rem(q, 2) == 0, k + 2 < half))(
+                lambda: self.step(k + 2, False)
+            )
+            pl.when(lax.rem(q, 2) == 1)(lambda: self.step(k + 1, True))
+            slot(q)
+
+        loop(0, 2 * (half - 1), body)
 
     def last(self, u):
         half = self.ring.half
@@ -329,7 +331,7 @@
 
 
 def interleaved(chips, sectors, local):
-    return chips == sectors and chips > 6 and local % 2 == 0
+    return chips == sectors and chips == 8 and local % 2 == 0
 
 
 def whole_kernel(
@@ -352,17 +354,16 @@
 
     keep = pltpu.make_async_copy(wave, g1.own(), loads.at[3])
     keep.start()
-    ring.barrier()
-    keep.wait()
-    for u in range(SUBS):
-        g1.start(u)
     loaded = [
         pltpu.make_async_copy(a, b, loads.at[i])
         for i, (a, b) in enumerate(((left_in, lefts), (tensor_in, tensor), (right_in, rights)))
     ]
     for copy in loaded:
         copy.start()
-
+    ring.barrier()
+    keep.wait()
+    for u in range(SUBS):
+        g1.start(u)
     def sector_of(i):
         return ring.chip_of(m - 1 - i) if tight else i
 
@@ -382,15 +383,6 @@
         crossing(i).wait_recv()
         n = m - 1 - i
         work.to(ring.chip_of(n), whole, lambda t: moved[i, t], s3, lambda: s3.offer(n))
-
-    def hops(st, low, high, slot):
-        def body(k):
-            pl.when(k > low)(
-                lambda: st.hop(1 + lax.div(k - low - 1, SUBS), lax.rem(k - low - 1, SUBS))
-            )
-            slot(k)
-
-        loop(low, high, body)
 
     def finish(st, ref, after=lambda u: None):
         size = rows // SUBS
@@ -403,60 +395,62 @@
 
     for copy in loaded:
         copy.wait()
-    steps = SUBS * (half - 1) + 1
     if tight:
-        def first_work(i, n, ready):
-            pl.when(jnp.logical_or(i == 0, jnp.logical_and(lax.rem(i, 2) == 1, i < m - 1)))(
+        def sectors_in(g, st, v, low, high):
+            def body(n):
+                g.ready(n)
+                apply_to(st, v, n)
+
+            lax.fori_loop(low, high, lambda n, c: body(n) or c, 0)
+
+        def first_work(i, low, high):
+            pl.when(jnp.logical_or(i == 0, jnp.logical_and(lax.rem(i, 2) == 1, i < m - 3)))(
                 lambda: renew_one(lax.div(i + 1, 2))
             )
-            ready()
-            pl.when(i != 1)(lambda: apply_to(s1, whole, n))
+            pl.when(i == m - 1)(lambda: s1.step(1, False))
+            sectors_in(g1, s1, whole, low, high)
 
         g1.run(first_work)
-        s1.first()
-
-        def first_slot(k):
-            pl.when(jnp.logical_and(k > 0, k <= half))(lambda: renew_one(half - 1 + k))
-            pl.when(jnp.logical_or(k == 0, jnp.logical_and(k > half, k <= half + 2)))(
-                lambda: apply_moved(jnp.maximum(k - half, 0))
+        s1.step(0, True)
+
+        def first_slot(q):
+            pl.when(q < half + 1)(lambda: renew_one(half - 1 + q))
+            pl.when(jnp.logical_or(q == 0, jnp.logical_or(q == 3, q == 4)))(
+                lambda: apply_moved(jnp.maximum(q - 2, 0))
             )
-            pl.when(k == 0)(s3.first)
-
-        hops(s1, 0, steps, first_slot)
-        for u in range(SUBS):
-            s3.hop(1, u)
+
+        s1.rest(first_slot, lambda q: pl.when(q == 5)(lambda: s3.step(0, True)))
+        s3.step(1, False)
         finish(s1, g2.own(), g2.start)
         write(0, g2.own(), out1)
 
-        def second_work(i, n, ready):
-            pl.when(i == m - 2)(lambda: [s3.hop(2, u) for u in range(SUBS)] and None)
-            ready()
-            pl.when(i != 1)(lambda: apply_to(s2, image, n))
-            pl.when(jnp.logical_and(lax.rem(i, 2) == 1, i < m - 1))(
-                lambda: apply_moved(3 + lax.div(i, 2))
-            )
+        def second_work(i, low, high):
+            def turn():
+                s3.step(1, True)
+                s3.step(2, False)
+
+            pl.when(i == m - 4)(turn)
+            pl.when(i == m - 1)(lambda: s2.step(1, False))
+            sectors_in(g2, s2, image, low, high)
+            pl.when(jnp.logical_or(i == 1, i == 3))(lambda: apply_moved(3 + lax.div(i, 2)))
 
         g2.run(second_work)
-        s2.first()
-        done = half + 2
-
-        def second_slot(k):
-            pl.when(jnp.logical_and(lax.rem(k, 2) == 0, k < 2 * (sectors - done)))(
-                lambda: apply_moved(done + lax.div(k, 2))
-            )
-            for j in range(3, half):
-                pl.when(k == max(2 * (2 * j - done) + 1, 1))(
-                    lambda j=j: [s3.hop(j, u) for u in range(SUBS)] and None
-                )
-
-        hops(s2, 0, steps, second_slot)
+        s2.step(0, True)
+        s3.step(2, True)
+
+        def second_slot(q):
+            pl.when(q == 2)(lambda: s3.step(3, False))
+            pl.when(q < 3)(lambda: apply_moved(5 + q))
+
+        s2.rest(second_slot, lambda q: pl.when(q == 5)(lambda: s3.step(3, True)))
         finish(s3, stage.at[1])
         write(2, stage.at[1], out3)
         finish(s2, stage.at[0])
         write(1, stage.at[0], out2)
     else:
-        def plain(i, n, ready):
-            ready()
+        def plain(g):
+            g.run(lambda i, low, high: None)
+            loop(0, m, g.ready)
 
         def spread(st, v, left_of, before=lambda q: None):
             def body(q):
@@ -465,18 +459,20 @@
 
             loop(0, sectors, body)
             loop(0, m, st.offer)
-            st.first()
-            hops(st, 0, steps, lambda k: None)
+            st.step(0, True)
+            if half > 1:
+                st.step(1, False)
+            st.rest(lambda q: None)
 
         def plain_left(q, t):
             return lefts[t, q]
 
         loop(0, sectors, renew_one)
-        g1.run(plain)
+        plain(g1)
         spread(s1, whole, plain_left)
         finish(s1, g2.own(), g2.start)
         write(0, g2.own(), out1)
-        g2.run(plain)
+        plain(g2)
         spread(s2, image, plain_left)
         finish(s2, stage.at[0])
         write(1, stage.at[0], out2)

time: 126 us -> 120 us (0.952)
  Pallas kernels: 125 us -> 119 us
    pallas_call x1, Pallas kernels: 123 us -> 117 us  [shards(): pl.pallas_call(functools.partial(whole_kernel, count, sections), out_shap...]
where the time goes in v2:
time: 120 us
  Pallas kernels  119 us (99%)
    pallas_call x1, Pallas kernels, shards(): pl.pallas_call(functools.partial(whole_kernel, count, sections), out_shap...  117 us

profile of v2, /device:TPU:0, one launch (start us, length us, event | category | flops | bytes accessed | tf_op | source)
XLA Modules:
  0.0 119.9 jit_solution(8302654012222446971)
XLA Ops:
  0.6 117.4 %images.1 = (bf16[512,256]{1,0:T(8,128)(2,1)}, bf16[512,256]{1,0:T(8,128)(2,1)}, bf16[512,256]{1,0:T(8,128)(2,1)}) custom-call(s32[1,8]{1,0:T(1,128)} %pair.1, s32[1,3]{1,0:T(1,128)} %limits.1, f32[1,3,4,4]{3,2,1,0:T(4,128)} %mixers.1, bf16[512,256]{1,0:T(8,128)(2,1)} %bitcast.10, bf16[3,8,256,256]{3,2,1,0:T(8,128)(2,1)} %bitcast.8, ...), custom_call_target="tpu_custom_call" | custom-call | tf_op jit(solution)/shard_map/images/pallas_call | solution.py:535
  118.1 1.9 %hand_out.1 = (bf16[512,256]{1,0:T(8,128)(2,1)}, bf16[512,256]{1,0:T(8,128)(2,1)}, bf16[512,256]{1,0:T(8,128)(2,1)}) custom-call(bf16[512,256]{1,0:T(8,128)(2,1)} %get-tuple-element.9.refs_0_, bf16[512,256]{1,0:T(8,128)(2,1)} %get-tuple-element.10.refs_1_, bf16[512,256]{1,0:T(8,128)(2,1)} %get-tuple-element.11.refs_2_), custom_call_target="tpu_custom_call" | custom-call | tf_op jit(solution)/shard_map/hand_out/pallas_call | solution.py:552

commit v3 on v2

--- a/solution.py
+++ b/solution.py
@@ -335,9 +335,9 @@
 
 
 def whole_kernel(
-    count, sections, pair, limits, mixers, wave, left_in, right_in, tensor_in,
+    count, sections, pair_in, limits_in, mixers_in, wave, left_in, right_in, tensor_in,
     out1, out2, out3,
-    lefts, rights, tensor, whole, image, renewed, moved, acc, stage,
+    pair, limits, mixers, lefts, rights, tensor, whole, image, renewed, moved, acc, stage,
     loads, writes, cross_send, cross_recv, *rest
 ):
     ring = Ring(count, sections)
@@ -354,6 +354,12 @@
 
     keep = pltpu.make_async_copy(wave, g1.own(), loads.at[3])
     keep.start()
+    scalars = [
+        pltpu.make_async_copy(a, b, loads.at[i])
+        for i, (a, b) in enumerate(((pair_in, pair), (limits_in, limits), (mixers_in, mixers)), 4)
+    ]
+    for copy in scalars:
+        copy.start()
     loaded = [
         pltpu.make_async_copy(a, b, loads.at[i])
         for i, (a, b) in enumerate(((left_in, lefts), (tensor_in, tensor), (right_in, rights)))
@@ -393,7 +399,7 @@
     def write(i, src, dst):
         pltpu.make_async_copy(src, dst, writes.at[i]).start()
 
-    for copy in loaded:
+    for copy in scalars + loaded:
         copy.wait()
     if tight:
         def sectors_in(g, st, v, low, high):
@@ -412,12 +418,11 @@
 
         g1.run(first_work)
         s1.step(0, True)
+        loop(0, 2, apply_moved)
 
         def first_slot(q):
             pl.when(q < half + 1)(lambda: renew_one(half - 1 + q))
-            pl.when(jnp.logical_or(q == 0, jnp.logical_or(q == 3, q == 4)))(
-                lambda: apply_moved(jnp.maximum(q - 2, 0))
-            )
+            pl.when(q == half + 1)(lambda: apply_moved(2))
 
         s1.rest(first_slot, lambda q: pl.when(q == 5)(lambda: s3.step(0, True)))
         s3.step(1, False)
@@ -527,7 +532,6 @@
     height = count * rows // sectors
     tight = interleaved(chips, sectors, site_ops.shape[2])
     dma = pltpu.SemaphoreType.DMA
-    sm = pl.BlockSpec(memory_space=pltpu.SMEM)
     anyw = pl.BlockSpec(memory_space=pl.ANY)
     image = pltpu.VMEM((sectors, height, width), BF)
     across = pltpu.VMEM((sectors, terms, block, block), BF)
@@ -535,14 +539,15 @@
     outs = pl.pallas_call(
         functools.partial(whole_kernel, count, sections),
         out_shape=[mine] * 3,
-        in_specs=[sm] * 3 + [anyw] * 4,
+        in_specs=[anyw] * 7,
         out_specs=[anyw] * 3,
         scratch_shapes=[
-            pltpu.VMEM(lefts.shape, BF), pltpu.VMEM(rights.shape, BF),
+            pltpu.SMEM(pairing.shape, jnp.int32), pltpu.SMEM(reach.shape, jnp.int32),
+            pltpu.SMEM(site_ops.shape, F32), pltpu.VMEM(lefts.shape, BF), pltpu.VMEM(rights.shape, BF),
             pltpu.VMEM(tensor.shape, BF), image, image, across, across,
             pltpu.VMEM((8, width) if tight else (height, width), F32),
             pltpu.VMEM((2, rows, width), BF),
-            dma((4,)), dma((3,)), dma((sectors,)), dma((sectors,)),
+            dma((7,)), dma((3,)), dma((sectors,)), dma((sectors,)),
         ] + scatter_scratch(chips, rows, width) * 3 + gather_scratch(chips // 2) * 2,
         compiler_params=pltpu.CompilerParams(
             collective_id=0, has_side_effects=True, vmem_limit_bytes=BIG

time: 120 us -> 117 us (0.975)
  Pallas kernels: 119 us -> 116 us
    pallas_call x1, Pallas kernels: 117 us -> 114 us  [shards(): pl.pallas_call(functools.partial(whole_kernel, count, sections), out_shap...]
where the time goes in v3:
time: 117 us
  Pallas kernels  116 us (99%)
    pallas_call x1, Pallas kernels, shards(): pl.pallas_call(functools.partial(whole_kernel, count, sections), out_shap...  114 us

profile of v3, /device:TPU:0, one launch (start us, length us, event | category | flops | bytes accessed | tf_op | source)
XLA Modules:
  0.0 116.8 jit_solution(4062468366410015022)
XLA Ops:
  0.6 114.2 %images.1 = (bf16[512,256]{1,0:T(8,128)(2,1)}, bf16[512,256]{1,0:T(8,128)(2,1)}, bf16[512,256]{1,0:T(8,128)(2,1)}) custom-call(s32[1,8]{1,0:T(1,128)} %pair_in.1, s32[1,3]{1,0:T(1,128)} %limits_in.1, f32[1,3,4,4]{3,2,1,0:T(4,128)} %mixers_in.1, bf16[512,256]{1,0:T(8,128)(2,1)} %bitcast.10, bf16[3,8,256,256]{3,2,1,0:T(8,128)(2,1)} %bitcast.8, ...), custom_call_target="tpu_custom_call" | custom-call | tf_op jit(solution)/shard_map/images/pallas_call | solution.py:539
  114.8 1.9 %hand_out.1 = (bf16[512,256]{1,0:T(8,128)(2,1)}, bf16[512,256]{1,0:T(8,128)(2,1)}, bf16[512,256]{1,0:T(8,128)(2,1)}) custom-call(bf16[512,256]{1,0:T(8,128)(2,1)} %get-tuple-element.9.refs_0_, bf16[512,256]{1,0:T(8,128)(2,1)} %get-tuple-element.10.refs_1_, bf16[512,256]{1,0:T(8,128)(2,1)} %get-tuple-element.11.refs_2_), custom_call_target="tpu_custom_call" | custom-call | tf_op jit(solution)/shard_map/hand_out/pallas_call | solution.py:557
